TPU v7x, 256 devices: a whole 4x4x8 slice. The times are simulated.
256 devices in a mesh: cuts: 4 (over y), blk: 64 (over x, z, core).
Axes of the slice: x: 4, y: 4, z: 8, core: 2. Of those that a mesh axis runs over, the one named last changes fastest.
Arguments:
- gap_load: float32 [4, 128, 2, 256, 128], P('cuts', 'blk'), may hold values from -24 to 24
- offsets: int32 [4, 128, 2], P('cuts', 'blk'), may hold values from -1 to 255, as said below
- corner_map: int32 [4, 128, 4], P('cuts', 'blk'), may hold values from -1 to 511, as said below
- flexibility: float32 [4, 128, 1024, 1024], P('cuts', 'blk'), may hold values from -0.5 to 4.5, as said below
- coupling: float32 [4, 128, 12, 1024], P('cuts', 'blk'), may hold values from -1.25 to 1.25
- corner_rows: float32 [4, 128, 12, 1536], P('cuts', 'blk'), may hold values from -0.1 to 1.1, as said below
Outputs:
- multipliers: float32 [4, 128, 2, 256, 128], P('cuts', 'blk')
- residual: float32 [4, 128, 2, 256, 128], P('cuts', 'blk')
Inputs may be any that keep to these rules, and one draw needn't show every extreme that they name: `offsets`: on an interface owned by a subdomain, the neighbour's dof k matches the owner's dof (k + offset) mod 256; -1 marks an interface without multipliers: the tunnel's far end, or one that touches an excavated subdomain. `corner_map`: entries k = 0, 1, 2, 3 are the corners at near-left, near-right, far-left, far-right. Entry 2 of subdomain (r, c) is never -1, and every node is entry 2 of exactly one subdomain; the same node is entry 3 of (r, (c - 1) mod 128) and, for r + 1 < 4, entries 0 of (r + 1, c) and 1 of (r + 1, (c - 1) mod 128), and no other entry. -1 marks a clamped corner at the tunnel's near end. `flexibility`: each block is symmetric positive definite. `corner_rows`: row 3 k + j of a subdomain is row 3 m + j of one symmetric positive definite matrix of order 3 * 512, with m = corner_map entry k; zero rows where that entry is -1.
All inputs are finite; a program needn't handle non-finite values.
Results may differ from a plain program's by a relative error of at most 0.00021.
Values sent between devices are 32-bit elements; how exact they have to be, the bound alone decides.
A program may use at most 64 MiB of HBM per device.

v0:
```python
import jax
import jax.numpy as jnp
from jax import lax
from jax.sharding import PartitionSpec as P

ITERS = 3
HIGH = lax.Precision.HIGHEST


def from_behind(value, axis, steps):
    count = lax.axis_size(axis)
    first, last = (max(0, -steps), min(count, count - steps))
    return lax.ppermute(value, axis, [(source, source + steps) for source in range(first, last)])


def passed_along(value, axis, steps):
    count = lax.axis_size(axis)
    pairs = [(source, (source + steps) % count) for source in range(count)]
    return lax.ppermute(value, axis, pairs)


def rotate(values, amounts, orient):
    face_size = values.shape[-2]
    indices = (jnp.arange(face_size, dtype=jnp.int32) + orient * amounts[..., None]) % face_size
    return jnp.take_along_axis(values, indices[..., None], axis=-2)


def corner_indices(corner_map, dof_count):
    spread = 3 * corner_map[..., None] + jnp.arange(3, dtype=jnp.int32)
    spread = jnp.where(corner_map[..., None] >= 0, spread, dof_count)
    return spread.reshape(corner_map.shape[0], corner_map.shape[1], 12)


def inner_sum(first, second):
    return jnp.sum(first * second, axis=(0, 1, 2, 3))


def squares(residual):
    return lax.psum(inner_sum(residual, residual), ("cuts", "blk"))


def per_device(gap_load, offsets, corner_map, flexibility, coupling, corner_rows):
    cycle_count, circ_count, _, face_size, load_count = gap_load.shape
    dof_count = corner_rows.shape[-1]
    active = (offsets >= 0).astype(jnp.float32)[..., None, None]
    corner_dofs = corner_indices(corner_map, dof_count)
    residual = gap_load * active
    multipliers = jnp.zeros_like(residual)
    direction = residual
    norm_now = squares(residual)
    for iteration in range(ITERS):
        sent_far = -rotate(direction[:, :, 0], offsets[:, :, 0], 1)
        sent_right = -rotate(direction[:, :, 1], offsets[:, :, 1], 1)
        edge_near = from_behind(sent_far[-1], "cuts", 1)
        edge_left = passed_along(sent_right[:, -1], "blk", 1)
        nearside = jnp.concatenate([edge_near[None], sent_far[:-1]], axis=0)
        leftside = jnp.concatenate([edge_left[:, None], sent_right[:, :-1]], axis=1)
        loads = jnp.stack([nearside, direction[:, :, 0], leftside, direction[:, :, 1]], axis=2)
        loads = loads.reshape(cycle_count, circ_count, 4 * face_size, load_count)
        operator_corner_terms = jnp.einsum("rcki,rcin->rckn", coupling, loads, precision=HIGH)
        partial_value = jnp.zeros((dof_count, load_count), jnp.float32)
        partial_value = partial_value.at[corner_dofs.reshape(-1)].add(
            operator_corner_terms.reshape(-1, load_count), mode="drop"
        )
        coarse = lax.psum(partial_value, ("cuts", "blk"))
        corner_values = jnp.einsum("rckm,mn->rckn", corner_rows, coarse, precision=HIGH)
        moved = jnp.einsum("rcij,rcjn->rcin", flexibility, loads, precision=HIGH)
        moved = moved + jnp.einsum("rcki,rckn->rcin", coupling, corner_values, precision=HIGH)
        moved = moved.reshape(cycle_count, circ_count, 4, face_size, load_count)
        from_far = from_behind(moved[0, :, 0], "cuts", -1)
        from_right = passed_along(moved[:, 0, 2], "blk", -1)
        far_near = jnp.concatenate([moved[1:, :, 0], from_far[None]], axis=0)
        right_left = jnp.concatenate([moved[:, 1:, 2], from_right[:, None]], axis=1)
        jump_far = moved[:, :, 1] - rotate(far_near, offsets[:, :, 0], -1)
        jump_right = moved[:, :, 3] - rotate(right_left, offsets[:, :, 1], -1)
        mapped = jnp.stack([jump_far, jump_right], axis=2) * active
        step_size = norm_now / lax.psum(inner_sum(direction, mapped), ("cuts", "blk"))
        multipliers = multipliers + step_size * direction
        residual = residual - step_size * mapped
        norm_next = squares(residual)
        direction = residual + norm_next / norm_now * direction
        norm_now = norm_next
    return (multipliers, residual)


def solution(mesh):
    in_specs = (
        P("cuts", "blk", None, None, None),
        P("cuts", "blk", None),
        P("cuts", "blk", None),
        P("cuts", "blk", None, None),
        P("cuts", "blk", None, None),
        P("cuts", "blk", None, None),
    )
    out_specs = (P("cuts", "blk", None, None, None), P("cuts", "blk", None, None, None))
    return jax.shard_map(
        per_device, mesh=mesh, in_specs=in_specs, out_specs=out_specs, check_vma=False
    )
```

profile of v0, /device:TPU:1, one launch (start us, length us, event | category | flops | bytes accessed | tf_op | source)
XLA Modules:
  0.0 1306.6 jit_solution(7525697432891195552)
XLA Ops:
  8.0 1.0 multiply_reduce_fusion.7
  9.2 1.1 copy_multiply_fusion
  10.4 3.7 gather_fusion.1
  14.3 3.1 collective-permute-start.1
  17.6 3.7 gather_fusion
  21.4 3.2 collective-permute-start
  25.0 4.6 collective-permute-done
  30.7 1.0 convolution_bitcast_fusion.5
  31.7 1.6 scatter_custom_fusion
  33.4 11.0 fusion.4
  44.4 248.0 %all-reduce.5.cloned.1.call-done = f32[1536,128]{1,0:T(8,128)} async-done(((f32[1536,128]{1,0:T(8,128)}), f32[1536,128]{1,0:T(8,128)}) %all-reduce.5.cloned.1.call-update) | async-done | bytes 786448 | tf_op jit(solution)/shard_map/psum | solution.py:65
  292.4 1.8 convolution_bitcast_fusion.4
  294.2 2.0 fusion.8
  296.2 1.7 reshape.723
  298.3 2.4 collective-permute-start.3
  301.8 1.3 collective-permute-start.2
  303.1 3.7 gather_fusion.3
  306.9 2.0 collective-permute-done.2
  308.9 3.7 gather_fusion.2
  312.9 78.9 %all-reduce = (f32[128]{0:T(128)S(1)}, f32[128]{0:T(128)S(1)}) all-reduce(f32[128]{0:T(128)S(1)} %get-tuple-element.8, f32[128]{0:T(128)S(1)} %get-tuple-element.7), channel_id=1, replica_groups=mesh['cuts'=4,'blk'=64] {'cuts','blk'}, use_global_device_ids=true, to_apply=%region_1.2 | all-reduce | flops 256 | bytes 2048 | tf_op jit(solution)/shard_map/psum | solution.py:39
  392.0 72.6 %psum.66 = f32[128]{0:T(128)S(1)} all-reduce(f32[128]{0:T(128)S(1)} %multiply_reduce_fusion.3), channel_id=1, replica_groups=mesh['cuts'=4,'blk'=64] {'cuts','blk'}, use_global_device_ids=true, to_apply=%region_7.9 | all-reduce | flops 128 | bytes 1024 | tf_op jit(solution)/shard_map/psum | solution.py:39
  464.9 3.7 gather_fusion.4
  468.7 3.7 gather_fusion.5
  472.5 2.4 collective-permute-start.4
  475.0 2.7 collective-permute-start.5
  477.7 1.9 collective-permute-done.5
  481.0 1.0 convolution_bitcast_fusion.3
  482.0 1.6 scatter_custom_fusion.1
  483.9 11.0 fusion.2
  494.9 243.5 %all-reduce.7.cloned.1.call-done = f32[1536,128]{1,0:T(8,128)} async-done(((f32[1536,128]{1,0:T(8,128)}), f32[1536,128]{1,0:T(8,128)}) %all-reduce.7.cloned.1.call-update) | async-done | bytes 786448 | tf_op jit(solution)/shard_map/psum | solution.py:65
  738.4 1.7 convolution_bitcast_fusion.2
  740.1 2.0 fusion.7
  742.1 1.7 reshape.726
  744.9 2.2 collective-permute-start.7
  748.1 1.3 collective-permute-start.6
  750.5 3.7 gather_fusion.7
  755.2 3.7 gather_fusion.6
  759.9 80.2 %psum.68 = f32[128]{0:T(128)S(1)} all-reduce(f32[128]{0:T(128)S(1)} %multiply_reduce_fusion.2), channel_id=1, replica_groups=mesh['cuts'=4,'blk'=64] {'cuts','blk'}, use_global_device_ids=true, to_apply=%region_11.13 | all-reduce | flops 128 | bytes 1024 | tf_op jit(solution)/shard_map/psum | solution.py:77
  840.9 72.8 %psum.69 = f32[128]{0:T(128)S(1)} all-reduce(f32[128]{0:T(128)S(1)} %get-tuple-element.15), channel_id=1, replica_groups=mesh['cuts'=4,'blk'=64] {'cuts','blk'}, use_global_device_ids=true, to_apply=%region_13.15 | all-reduce | flops 128 | bytes 1024 | tf_op jit(solution)/shard_map/psum | solution.py:39
  915.3 3.7 gather_fusion.8
  919.8 3.7 gather_fusion.9
  923.6 2.2 collective-permute-start.8
  925.8 2.7 collective-permute-start.9
  928.5 1.9 collective-permute-done.9
  930.8 1.3 copy.59
  932.2 1.8 reshape.727
  934.0 1.0 convolution_bitcast_fusion.1
  935.0 1.7 scatter_custom_fusion.2
  936.7 12.0 fusion
  948.8 242.0 %all-reduce.9.cloned.1.call-done = f32[1536,128]{1,0:T(8,128)} async-done(((f32[1536,128]{1,0:T(8,128)}), f32[1536,128]{1,0:T(8,128)}) %all-reduce.9.cloned.1.call-update) | async-done | bytes 786448 | tf_op jit(solution)/shard_map/psum | solution.py:65
  1190.8 1.7 convolution_bitcast_fusion
  1192.5 3.3 fusion.6
  1195.8 1.7 reshape.729
  1198.5 1.7 copy.88
  1200.1 2.3 collective-permute-start.11
  1202.4 1.5 fusion.46
  1203.9 1.8 copy.85
  1205.7 1.8 copy.86
  1207.5 1.1 copy.84
  1208.6 1.3 collective-permute-start.10
  1210.8 3.7 gather_fusion.11
  1214.5 1.1 fusion.18
  1215.9 3.7 gather_fusion.10
  1220.0 77.9 %psum.71 = f32[128]{0:T(128)S(1)} all-reduce(f32[128]{0:T(128)S(1)} %multiply_reduce_fusion), channel_id=1, replica_groups=mesh['cuts'=4,'blk'=64] {'cuts','blk'}, use_global_device_ids=true, to_apply=%region_17.19 | all-reduce | flops 128 | bytes 1024 | tf_op jit(solution)/shard_map/psum | solution.py:77
  (129 shorter events, 21.0 us)
Async XLA Ops:
  7.2 285.2 %copy-start = (f32[1,2,12,1536]{3,1,2,0:T(2,128)S(1)}, f32[1,2,12,1536]{3,1,2,0:T(2,128)}, u32[]{:S(2)}) copy-start(f32[1,2,12,1536]{3,1,2,0:T(2,128)} %param.13) | copy-start | bytes 442372
  7.2 17.4 %copy-start.12 = (s32[1,2,4]{2,1,0:T(2,128)S(1)}, s32[1,2,4]{2,1,0:T(2,128)}, u32[]{:S(2)}) copy-start(s32[1,2,4]{2,1,0:T(2,128)} %param.10) | copy-start | bytes 100
  7.2 23.5 %copy-start.2 = (f32[1,2,12,1024]{3,1,2,0:T(2,128)S(1)}, f32[1,2,12,1024]{3,1,2,0:T(2,128)}, u32[]{:S(2)}) copy-start(f32[1,2,12,1024]{3,1,2,0:T(2,128)} %param.12) | copy-start | bytes 294916
  7.2 285.2 %all-reduce.5.cloned.1.call-start = ((), (), s32[]{:S(2)}) async-start(), calls=%async_computation | async-start | bytes 1572864 | tf_op jit(solution)/shard_map/psum | solution.py:65
  9.0 463.4 %copy-start.5 = (pred[2,256]{1,0:T(4,128)(4,1)}, pred[2,256]{1,0:T(4,128)(4,1)S(1)}, u32[]{:S(2)}) copy-start(pred[2,256]{1,0:T(4,128)(4,1)S(1)} %and_bitcast_fusion.2) | copy-start | bytes 1540
  14.3 10.7 collective-permute-start.1
  17.5 451.1 %copy-start.7 = (pred[2,256]{1,0:T(4,128)(4,1)}, pred[2,256]{1,0:T(4,128)(4,1)S(1)}, u32[]{:S(2)}) copy-start(pred[2,256]{1,0:T(4,128)(4,1)S(1)} %and_bitcast_fusion.3) | copy-start | bytes 1540
  21.4 8.3 collective-permute-start
  25.0 457.0 %copy-start.13 = (s32[24]{0:T(128)}, s32[24]{0:T(128)S(1)}, u32[]{:S(2)}) copy-start(s32[24]{0:T(128)S(1)} %fusion.45) | copy-start | bytes 292
  33.3 705.1 %all-reduce.7.cloned.1.call-start = ((), (), s32[]{:S(2)}) async-start(), calls=%async_computation.1 | async-start | bytes 1572864 | tf_op jit(solution)/shard_map/psum | solution.py:65
  292.4 20.3 %copy-start.1 = (f32[1,2,2,256,128]{4,3,2,1,0:T(8,128)S(1)}, f32[1,2,2,256,128]{4,3,2,1,0:T(8,128)}, u32[]{:S(2)}) copy-start(f32[1,2,2,256,128]{4,3,2,1,0:T(8,128)} %param.8) | copy-start | bytes 1572868
  298.3 4.8 collective-permute-start.3
  301.8 7.1 collective-permute-start.2
  464.6 16.3 %copy-start.14 = (f32[128]{0:T(128)}, f32[128]{0:T(128)S(1)}, u32[]{:S(2)}) copy-start(f32[128]{0:T(128)S(1)} %psum.66) | copy-start | bytes 1540
  464.6 16.3 %copy-start.8 = (f32[128]{0:T(128)}, f32[128]{0:T(128)S(1)}, u32[]{:S(2)}) copy-start(f32[128]{0:T(128)S(1)} %div.16) | copy-start | bytes 1540
  472.5 7.4 collective-permute-start.4
  475.0 4.6 collective-permute-start.5
  483.6 707.2 %all-reduce.9.cloned.1.call-start = ((), (), s32[]{:S(2)}) async-start(), calls=%async_computation.2 | async-start | bytes 1572864 | tf_op jit(solution)/shard_map/psum | solution.py:65
  744.9 4.7 collective-permute-start.7
  748.1 7.1 collective-permute-start.6
  755.2 168.2 %copy-start.6 = (pred[2,256]{1,0:T(4,128)(4,1)S(1)}, pred[2,256]{1,0:T(4,128)(4,1)}, u32[]{:S(2)}) copy-start(pred[2,256]{1,0:T(4,128)(4,1)} %copy-done.5) | copy-start | bytes 1540
  840.7 91.5 %copy-start.10 = (f32[128]{0:T(128)}, f32[128]{0:T(128)S(1)}, u32[]{:S(2)}) copy-start(f32[128]{0:T(128)S(1)} %div.17) | copy-start | bytes 1540
  840.9 73.4 %copy-start.3 = (f32[1,2,2,256,128]{4,3,1,2,0:T(8,128)}, f32[1,2,2,256,128]{4,3,1,2,0:T(8,128)S(1)}, u32[]{:S(2)}) copy-start(f32[1,2,2,256,128]{4,3,1,2,0:T(8,128)S(1)} %get-tuple-element.16) | copy-start | bytes 1572868
  913.7 20.2 %copy-start.15 = (f32[128]{0:T(128)}, f32[128]{0:T(128)S(1)}, u32[]{:S(2)}) copy-start(f32[128]{0:T(128)S(1)} %psum.69) | copy-start | bytes 1540
  923.6 7.2 collective-permute-start.8
  925.8 4.6 collective-permute-start.9
  1192.5 105.4 %copy-start.4 = (f32[1,2,2,256,128]{4,3,1,2,0:T(8,128)S(1)}, f32[1,2,2,256,128]{4,3,1,2,0:T(8,128)}, u32[]{:S(2)}) copy-start(f32[1,2,2,256,128]{4,3,1,2,0:T(8,128)} %copy-done.3) | copy-start | bytes 1572868
  1192.5 105.4 %copy-start.9 = (f32[128]{0:T(128)S(1)}, f32[128]{0:T(128)}, u32[]{:S(2)}) copy-start(f32[128]{0:T(128)} %copy-done.8) | copy-start | bytes 1540
  1192.5 105.4 %copy-start.11 = (f32[128]{0:T(128)S(1)}, f32[128]{0:T(128)}, u32[]{:S(2)}) copy-start(f32[128]{0:T(128)} %copy-done.10) | copy-start | bytes 1540
  1195.8 102.1 %copy-start.16 = (f32[128]{0:T(128)S(1)}, f32[128]{0:T(128)}, u32[]{:S(2)}) copy-start(f32[128]{0:T(128)} %copy-done.15) | copy-start | bytes 1540
  1200.1 9.8 collective-permute-start.11
  1208.6 7.3 collective-permute-start.10
Sparse Core Ops, SparseCore 0:
  33.4 258.9 all-reduce.4
  483.7 254.6 all-reduce.6
  936.8 253.8 all-reduce.8
where the time goes:
time: 1320 us; the launch traced here: 1310 us
  waiting for transfers between devices  746 us (57%)
  blocking collectives  382 us (29%)
  local copies, waits for them, and re-layouts  68.4 us (5%)
  matrix products  49.6 us (4%)
  starting transfers between devices  27.4 us (2%)
  other arithmetic  18.2 us (1%)
  between operations  14.7 us (1%)
    psum x3, waiting for transfers between devices, per_device(): coarse = lax.psum(partial_value, ('cuts', 'blk'))  733 us
    psum x3, blocking collectives, squares(): return lax.psum(inner_sum(residual, residual), ('cuts', 'blk'))  224 us
    psum x2, blocking collectives, per_device(): lax.psum(inner_sum(direction, mapped), ('cuts', 'blk'))  158 us
    gather x12, local copies, waits for them, and re-layouts, rotate(): return jnp.take_along_axis(values, indices[..., None], axis=-2)  43.9 us
    dot_general x3, matrix products, per_device(): moved = jnp.einsum('rcij,rcjn->rcin', flexibility, loads, precision=HIGH)  34.1 us
  transfers between devices with their start and end apart: 15, of which 12 were waited for; matrix products, arithmetic and copies ran while one was open for 5% of the time, Pallas kernels for 0%

commit v1 on v0

--- a/solution.py
+++ b/solution.py
@@ -74,7 +74,12 @@
         jump_far = moved[:, :, 1] - rotate(far_near, offsets[:, :, 0], -1)
         jump_right = moved[:, :, 3] - rotate(right_left, offsets[:, :, 1], -1)
         mapped = jnp.stack([jump_far, jump_right], axis=2) * active
-        step_size = norm_now / lax.psum(inner_sum(direction, mapped), ("cuts", "blk"))
+
+        def resolve_zones_on(vec):
+            oldest = jax.lax.psum(jax.lax.psum(vec, "blk"), "cuts")
+            return oldest
+
+        step_size = norm_now / resolve_zones_on(inner_sum(direction, mapped))
         multipliers = multipliers + step_size * direction
         residual = residual - step_size * mapped
         norm_next = squares(residual)

time: 1320 us -> 1570 us (1.19)
  blocking collectives: 382 us -> 636 us
    psum x2 -> x6, blocking collectives: 158 us -> 407 us  [resolve_zones_on(): oldest = jax.lax.psum(jax.lax.psum(vec, 'blk'), 'cuts')]
  transfers between devices with their start and end apart: 15 -> 15, of which waited for: 12 -> 12; matrix products, arithmetic and copies ran while one was open for 5% -> 4% of each run, Pallas kernels for 0% -> 0%
where the time goes in v1:
time: 1570 us; the launch traced here: 1560 us
  waiting for transfers between devices  744 us (47%)
  blocking collectives  636 us (41%)
  local copies, waits for them, and re-layouts  68.4 us (4%)
  matrix products  49.6 us (3%)
  starting transfers between devices  28.2 us (2%)
  other arithmetic  18.2 us (1%)
    psum x3, waiting for transfers between devices, per_device(): coarse = lax.psum(partial_value, ('cuts', 'blk'))  730 us
    psum x6, blocking collectives, resolve_zones_on(): oldest = jax.lax.psum(jax.lax.psum(vec, 'blk'), 'cuts')  407 us
    psum x3, blocking collectives, squares(): return lax.psum(inner_sum(residual, residual), ('cuts', 'blk'))  228 us
    gather x12, local copies, waits for them, and re-layouts, rotate(): return jnp.take_along_axis(values, indices[..., None], axis=-2)  43.9 us
    dot_general x3, matrix products, per_device(): moved = jnp.einsum('rcij,rcjn->rcin', flexibility, loads, precision=HIGH)  34.1 us
  transfers between devices with their start and end apart: 15, of which 12 were waited for; matrix products, arithmetic and copies ran while one was open for 4% of the time, Pallas kernels for 0%

profile of v1, /device:TPU:1, one launch (start us, length us, event | category | flops | bytes accessed | tf_op | source)
XLA Modules:
  0.0 1558.9 jit_solution(14081481286458546857)
XLA Ops:
  9.2 1.1 copy_multiply_fusion
  10.4 3.7 gather_fusion.1
  14.3 3.1 collective-permute-start.1
  17.6 3.7 gather_fusion
  21.4 3.2 collective-permute-start
  25.0 4.6 collective-permute-done
  31.7 1.6 scatter_custom_fusion
  33.4 11.0 fusion.4
  44.4 248.0 %all-reduce.4.cloned.1.call-done = f32[1536,128]{1,0:T(8,128)} async-done(((f32[1536,128]{1,0:T(8,128)}), f32[1536,128]{1,0:T(8,128)}) %all-reduce.4.cloned.1.call-update) | async-done | bytes 786448 | tf_op jit(solution)/shard_map/psum | solution.py:65
  292.4 1.8 convolution_bitcast_fusion.4
  294.2 2.0 fusion.8
  296.2 1.7 reshape.723
  298.3 2.4 collective-permute-start.3
  301.7 1.3 collective-permute-start.2
  303.1 3.7 gather_fusion.3
  306.9 2.0 collective-permute-done.2
  308.9 3.7 gather_fusion.2
  312.9 128.0 %psum.86 = f32[128]{0:T(128)S(1)} all-reduce(f32[128]{0:T(128)S(1)} %get-tuple-element.7), channel_id=1, replica_groups=mesh['cuts'=4,'blk'=64] {'blk'}, use_global_device_ids=true, to_apply=%region_5.7 | all-reduce | flops 128 | bytes 1024 | tf_op jit(solution)/shard_map/psum | solution.py:79
  440.9 7.2 psum.87
  448.1 76.6 %psum.84 = f32[128]{0:T(128)S(1)} all-reduce(f32[128]{0:T(128)S(1)} %get-tuple-element.8), channel_id=1, replica_groups=mesh['cuts'=4,'blk'=64] {'cuts','blk'}, use_global_device_ids=true, to_apply=%region_1.2 | all-reduce | flops 128 | bytes 1024 | tf_op jit(solution)/shard_map/psum | solution.py:39
  524.8 74.4 %psum.88 = f32[128]{0:T(128)S(1)} all-reduce(f32[128]{0:T(128)S(1)} %multiply_reduce_fusion.3), channel_id=1, replica_groups=mesh['cuts'=4,'blk'=64] {'cuts','blk'}, use_global_device_ids=true, to_apply=%region_8.10 | all-reduce | flops 128 | bytes 1024 | tf_op jit(solution)/shard_map/psum | solution.py:39
  599.5 3.7 gather_fusion.4
  603.3 3.7 gather_fusion.5
  607.1 3.0 collective-permute-start.4
  610.2 1.8 collective-permute-start.5
  612.0 1.9 collective-permute-done.5
  614.0 1.1 collective-permute-done.4
  617.2 1.6 scatter_custom_fusion.1
  619.1 11.0 fusion.2
  630.1 241.5 %all-reduce.6.cloned.1.call-done = f32[1536,128]{1,0:T(8,128)} async-done(((f32[1536,128]{1,0:T(8,128)}), f32[1536,128]{1,0:T(8,128)}) %all-reduce.6.cloned.1.call-update) | async-done | bytes 786448 | tf_op jit(solution)/shard_map/psum | solution.py:65
  871.6 1.7 convolution_bitcast_fusion.2
  873.3 2.0 fusion.7
  875.4 1.7 reshape.726
  878.1 2.1 collective-permute-start.7
  881.3 1.3 collective-permute-start.6
  883.7 3.7 gather_fusion.7
  888.4 3.7 gather_fusion.6
  893.1 128.0 %psum.90 = f32[128]{0:T(128)S(1)} all-reduce(f32[128]{0:T(128)S(1)} %multiply_reduce_fusion.2), channel_id=1, replica_groups=mesh['cuts'=4,'blk'=64] {'blk'}, use_global_device_ids=true, to_apply=%region_12.14 | all-reduce | flops 128 | bytes 1024 | tf_op jit(solution)/shard_map/psum | solution.py:79
  1021.1 7.7 psum.91
  1029.7 77.5 %psum.92 = f32[128]{0:T(128)S(1)} all-reduce(f32[128]{0:T(128)S(1)} %get-tuple-element.13), channel_id=1, replica_groups=mesh['cuts'=4,'blk'=64] {'cuts','blk'}, use_global_device_ids=true, to_apply=%region_15.17 | all-reduce | flops 128 | bytes 1024 | tf_op jit(solution)/shard_map/psum | solution.py:39
  1108.8 3.7 gather_fusion.8
  1113.3 3.7 gather_fusion.9
  1117.1 3.2 collective-permute-start.8
  1120.3 2.7 collective-permute-start.9
  1123.0 1.9 collective-permute-done.9
  1125.3 1.3 copy.59
  1126.7 1.8 reshape.727
  1129.4 1.7 scatter_custom_fusion.2
  1131.2 12.0 fusion
  1143.2 240.9 %all-reduce.8.cloned.1.call-done = f32[1536,128]{1,0:T(8,128)} async-done(((f32[1536,128]{1,0:T(8,128)}), f32[1536,128]{1,0:T(8,128)}) %all-reduce.8.cloned.1.call-update) | async-done | bytes 786448 | tf_op jit(solution)/shard_map/psum | solution.py:65
  1384.2 1.7 convolution_bitcast_fusion
  1385.9 3.3 fusion.6
  1389.2 1.7 reshape.729
  1391.8 1.7 copy.88
  1393.5 2.4 collective-permute-start.11
  1395.9 1.5 fusion.46
  1397.4 1.8 copy.85
  1399.3 1.8 copy.86
  1402.1 1.3 collective-permute-start.10
  1404.4 3.7 gather_fusion.11
  1408.0 1.1 fusion.18
  1409.5 3.7 gather_fusion.10
  1413.5 128.0 %psum.94 = f32[128]{0:T(128)S(1)} all-reduce(f32[128]{0:T(128)S(1)} %multiply_reduce_fusion), channel_id=1, replica_groups=mesh['cuts'=4,'blk'=64] {'blk'}, use_global_device_ids=true, to_apply=%region_19.21 | all-reduce | flops 128 | bytes 1024 | tf_op jit(solution)/shard_map/psum | solution.py:79
  1541.4 8.4 psum.95
  (133 shorter events, 25.7 us)
Async XLA Ops:
  7.2 285.2 %copy-start = (f32[1,2,12,1536]{3,1,2,0:T(2,128)S(1)}, f32[1,2,12,1536]{3,1,2,0:T(2,128)}, u32[]{:S(2)}) copy-start(f32[1,2,12,1536]{3,1,2,0:T(2,128)} %param.13) | copy-start | bytes 442372
  7.2 17.4 %copy-start.12 = (s32[1,2,4]{2,1,0:T(2,128)S(1)}, s32[1,2,4]{2,1,0:T(2,128)}, u32[]{:S(2)}) copy-start(s32[1,2,4]{2,1,0:T(2,128)} %param.10) | copy-start | bytes 100
  7.2 23.5 %copy-start.2 = (f32[1,2,12,1024]{3,1,2,0:T(2,128)S(1)}, f32[1,2,12,1024]{3,1,2,0:T(2,128)}, u32[]{:S(2)}) copy-start(f32[1,2,12,1024]{3,1,2,0:T(2,128)} %param.12) | copy-start | bytes 294916
  7.2 285.2 %all-reduce.4.cloned.1.call-start = ((), (), s32[]{:S(2)}) async-start(), calls=%async_computation | async-start | bytes 1572864 | tf_op jit(solution)/shard_map/psum | solution.py:65
  9.0 598.0 %copy-start.5 = (pred[2,256]{1,0:T(4,128)(4,1)}, pred[2,256]{1,0:T(4,128)(4,1)S(1)}, u32[]{:S(2)}) copy-start(pred[2,256]{1,0:T(4,128)(4,1)S(1)} %and_bitcast_fusion.2) | copy-start | bytes 1540
  14.3 10.7 collective-permute-start.1
  17.5 585.7 %copy-start.7 = (pred[2,256]{1,0:T(4,128)(4,1)}, pred[2,256]{1,0:T(4,128)(4,1)S(1)}, u32[]{:S(2)}) copy-start(pred[2,256]{1,0:T(4,128)(4,1)S(1)} %and_bitcast_fusion.3) | copy-start | bytes 1540
  21.4 8.3 collective-permute-start
  25.0 592.2 %copy-start.13 = (s32[24]{0:T(128)}, s32[24]{0:T(128)S(1)}, u32[]{:S(2)}) copy-start(s32[24]{0:T(128)S(1)} %fusion.45) | copy-start | bytes 292
  33.3 838.3 %all-reduce.6.cloned.1.call-start = ((), (), s32[]{:S(2)}) async-start(), calls=%async_computation.1 | async-start | bytes 1572864 | tf_op jit(solution)/shard_map/psum | solution.py:65
  292.4 20.3 %copy-start.1 = (f32[1,2,2,256,128]{4,3,2,1,0:T(8,128)S(1)}, f32[1,2,2,256,128]{4,3,2,1,0:T(8,128)}, u32[]{:S(2)}) copy-start(f32[1,2,2,256,128]{4,3,2,1,0:T(8,128)} %param.8) | copy-start | bytes 1572868
  298.3 4.8 collective-permute-start.3
  301.7 7.1 collective-permute-start.2
  599.2 15.9 %copy-start.14 = (f32[128]{0:T(128)}, f32[128]{0:T(128)S(1)}, u32[]{:S(2)}) copy-start(f32[128]{0:T(128)S(1)} %psum.88) | copy-start | bytes 1540
  599.2 15.9 %copy-start.8 = (f32[128]{0:T(128)}, f32[128]{0:T(128)S(1)}, u32[]{:S(2)}) copy-start(f32[128]{0:T(128)S(1)} %div.16) | copy-start | bytes 1540
  607.1 8.0 collective-permute-start.4
  610.2 3.8 collective-permute-start.5
  618.8 765.4 %all-reduce.8.cloned.1.call-start = ((), (), s32[]{:S(2)}) async-start(), calls=%async_computation.2 | async-start | bytes 1572864 | tf_op jit(solution)/shard_map/psum | solution.py:65
  878.1 4.7 collective-permute-start.7
  881.3 7.1 collective-permute-start.6
  888.4 228.5 %copy-start.6 = (pred[2,256]{1,0:T(4,128)(4,1)S(1)}, pred[2,256]{1,0:T(4,128)(4,1)}, u32[]{:S(2)}) copy-start(pred[2,256]{1,0:T(4,128)(4,1)} %copy-done.5) | copy-start | bytes 1540
  1029.4 97.2 %copy-start.10 = (f32[128]{0:T(128)}, f32[128]{0:T(128)S(1)}, u32[]{:S(2)}) copy-start(f32[128]{0:T(128)S(1)} %div.17) | copy-start | bytes 1540
  1029.7 78.2 %copy-start.3 = (f32[1,2,2,256,128]{4,3,1,2,0:T(8,128)}, f32[1,2,2,256,128]{4,3,1,2,0:T(8,128)S(1)}, u32[]{:S(2)}) copy-start(f32[1,2,2,256,128]{4,3,1,2,0:T(8,128)S(1)} %get-tuple-element.14) | copy-start | bytes 1572868
  1107.2 21.2 %copy-start.15 = (f32[128]{0:T(128)}, f32[128]{0:T(128)S(1)}, u32[]{:S(2)}) copy-start(f32[128]{0:T(128)S(1)} %psum.92) | copy-start | bytes 1540
  1117.1 8.2 collective-permute-start.8
  1120.3 4.6 collective-permute-start.9
  1385.9 164.0 %copy-start.4 = (f32[1,2,2,256,128]{4,3,1,2,0:T(8,128)S(1)}, f32[1,2,2,256,128]{4,3,1,2,0:T(8,128)}, u32[]{:S(2)}) copy-start(f32[1,2,2,256,128]{4,3,1,2,0:T(8,128)} %copy-done.3) | copy-start | bytes 1572868
  1385.9 164.0 %copy-start.9 = (f32[128]{0:T(128)S(1)}, f32[128]{0:T(128)}, u32[]{:S(2)}) copy-start(f32[128]{0:T(128)} %copy-done.8) | copy-start | bytes 1540
  1385.9 164.0 %copy-start.11 = (f32[128]{0:T(128)S(1)}, f32[128]{0:T(128)}, u32[]{:S(2)}) copy-start(f32[128]{0:T(128)} %copy-done.10) | copy-start | bytes 1540
  1389.2 160.7 %copy-start.16 = (f32[128]{0:T(128)S(1)}, f32[128]{0:T(128)}, u32[]{:S(2)}) copy-start(f32[128]{0:T(128)} %copy-done.15) | copy-start | bytes 1540
  1393.5 9.9 collective-permute-start.11
  1402.1 7.3 collective-permute-start.10
Sparse Core Ops, SparseCore 0:
  33.4 258.9 all-reduce.3
  618.9 252.6 all-reduce.5
  1131.3 252.7 all-reduce.7
